TPU v7x, 256 devices: a whole 4x4x8 slice. The times are simulated.
256 devices in a mesh: dp: 16 (over x, y_lo, core), fsdp: 16 (over z, y_hi).
Axes of the slice: x: 4, y: 4 (y_hi: 2, y_lo: 2; y = y_hi * 2 + y_lo), z: 8, core: 2. Of those that a mesh axis runs over, the one named last changes fastest.
Arguments:
- fields: bfloat16 [16, 6, 48, 48, 48, 128], P('dp', None, 'fsdp'), may hold values from -6 to 6
- targets: bfloat16 [16, 6, 48, 2304], P('dp', None, 'fsdp'), may hold values from -6 to 6
- lists: int32 [16, 6], P('dp'), may hold values from 0 to 5, each once within a row
- counts: int32 [16], replicated, may hold values from 1 to 6, as said below
- spectral_w: bfloat16 [32, 2, 128, 128], P('fsdp'), may hold values from -0.375 to 0.375
- local_w: bfloat16 [128, 128], replicated, may hold values from -0.5 to 0.5
- proj: float32 [128], replicated, may hold values from -0.5 to 0.5
Outputs:
- grad_spectral: float32 [32, 2, 128, 128], P('fsdp')
- grad_local: float32 [128, 128], replicated
Inputs may be any that keep to these rules, and one draw needn't show every extreme that they name: Each row of lists names every slot of its lane once; the first counts[l] entries of row l are lane l's live grids. `counts`: exactly one lane has 6 live grids; every other lane has 1 or 2.
All inputs are finite; a program needn't handle non-finite values.
Results may differ from a plain program's by a relative error of at most 0.0036.
The roundings to bfloat16 on the way count: a program that leaves them out, or rounds other values in their place, can miss the bound.
Values may be sent and summed in bfloat16 or wider, within the bound.
A program may use at most 64 MiB of HBM per device.

v0:
```python
import math

import jax
import jax.numpy as jnp
from jax import lax
from jax.sharding import PartitionSpec as P

MX = 4
MY = 4
MZ = 2


highest = lax.Precision.HIGHEST
root_half = 0.7071067811865476
inv_root_two_pi = 0.3989422804014327


def phase_table(mode_ids, cell_ids, length, direction):
    product = mode_ids[:, None] * cell_ids[None, :] % length
    angle = product.astype(jnp.float32) * (2.0 * math.pi / length)
    return (jnp.cos(angle), direction * jnp.sin(angle))


def mode_lists():
    kx_ids = jnp.arange(MX, dtype=jnp.int32) - MX // 2
    ky_ids = jnp.arange(MY, dtype=jnp.int32) - MY // 2
    kz_ids = jnp.arange(MZ, dtype=jnp.int32)
    return (kx_ids, ky_ids, kz_ids)


def complex_contract(real_part, imag_part, cos_t, sin_t, form):

    def product(left, right):
        return jnp.einsum(form, left, right, precision=highest)

    return (
        product(real_part, cos_t) - product(imag_part, sin_t),
        product(real_part, sin_t) + product(imag_part, cos_t),
    )


def forward_modes(grid_field, x_cells, scale):
    grid_len = grid_field.shape[1]
    kx_ids, ky_ids, kz_ids = mode_lists()
    cells = jnp.arange(grid_len, dtype=jnp.int32)
    cos_z, sin_z = phase_table(kz_ids, cells, grid_len, -1.0)
    part_re = jnp.einsum(
        "abzc,kz->abkc", grid_field, cos_z.astype(jnp.bfloat16), preferred_element_type=jnp.float32
    )
    part_im = jnp.einsum(
        "abzc,kz->abkc", grid_field, sin_z.astype(jnp.bfloat16), preferred_element_type=jnp.float32
    )
    cos_y, sin_y = phase_table(ky_ids, cells, grid_len, -1.0)
    next_re, next_im = complex_contract(part_re, part_im, cos_y, sin_y, "abkc,jb->ajkc")
    cos_x, sin_x = phase_table(kx_ids, x_cells, grid_len, -1.0)
    last_re, last_im = complex_contract(next_re, next_im, cos_x, sin_x, "ajkc,ia->ijkc")
    stacked = jnp.stack([last_re, last_im], axis=3) * scale
    return stacked.reshape(MX * MY * MZ, 2, stacked.shape[-1])


def inverse_modes(spectrum, x_cells, grid_len):
    kx_ids, ky_ids, kz_ids = mode_lists()
    cells = jnp.arange(grid_len, dtype=jnp.int32)
    values = spectrum.astype(jnp.float32).reshape(MX, MY, MZ, 2, spectrum.shape[-1])
    cos_x, sin_x = phase_table(kx_ids, x_cells, grid_len, 1.0)
    first_re, first_im = complex_contract(
        values[:, :, :, 0], values[:, :, :, 1], cos_x, sin_x, "ijkc,ia->ajkc"
    )
    cos_y, sin_y = phase_table(ky_ids, cells, grid_len, 1.0)
    second_re, second_im = complex_contract(first_re, first_im, cos_y, sin_y, "ajkc,jb->abkc")
    cos_z, sin_z = phase_table(kz_ids, cells, grid_len, 1.0)
    real_out = jnp.einsum("abkc,kz->abzc", second_re, cos_z, precision=highest)
    real_out = real_out - jnp.einsum("abkc,kz->abzc", second_im, sin_z, precision=highest)
    return real_out * float(MX * MY * MZ) ** (-0.5)


def mix_modes(coeff_b, weights):
    signs = jnp.array([1.0, -1.0], jnp.bfloat16).reshape(1, 2, 1, 1)
    spec_re = jnp.einsum(
        "gmri,mrio->gmo", coeff_b, weights * signs, preferred_element_type=jnp.float32
    )
    spec_im = jnp.einsum(
        "gmri,mrio->gmo", coeff_b[:, :, ::-1], weights, preferred_element_type=jnp.float32
    )
    return jnp.stack([spec_re, spec_im], axis=2)


def weight_grad(coeff_b, back_stack):
    coeff_f = coeff_b.astype(jnp.float32)
    rotated = jnp.stack([-coeff_f[:, :, 1], coeff_f[:, :, 0]], axis=2)
    grad_re = jnp.einsum("gmri,gmro->mio", coeff_f, back_stack, precision=highest)
    grad_im = jnp.einsum("gmri,gmro->mio", rotated, back_stack, precision=highest)
    return jnp.stack([grad_re, grad_im], axis=1)


def point_part(grid_field, branch, local_w, proj, grid_target, scale):
    width = grid_field.shape[-1]
    flat_field = grid_field.reshape(-1, width)
    pre = branch.reshape(-1, width) + jnp.dot(
        flat_field, local_w, preferred_element_type=jnp.float32
    )
    erf_part = lax.erf(pre * root_half)
    active = 0.5 * pre * (1.0 + erf_part)
    pred = jnp.dot(active, proj, precision=highest)
    resid = (pred - grid_target.reshape(-1).astype(jnp.float32)) * scale
    slope = 0.5 * (1.0 + erf_part) + pre * jnp.exp(-0.5 * pre * pre) * inv_root_two_pi
    d_pre = (resid[:, None] * proj[None, :] * slope).astype(jnp.bfloat16)
    local_grad = lax.dot_general(
        flat_field, d_pre, (((0,), (0,)), ((), ())), preferred_element_type=jnp.float32
    )
    return (d_pre.reshape(grid_field.shape), local_grad)


def body(fields, targets, lists, counts, spectral_w, local_w, proj):
    grid_store = fields[0]
    target_store = targets[0]
    slot_order = lists[0]
    slot_count = grid_store.shape[0]
    plane_count = grid_store.shape[1]
    grid_len = grid_store.shape[2]
    width = grid_store.shape[-1]
    lane_index = lax.axis_index("dp")
    x_cells = lax.axis_index("fsdp") * plane_count + jnp.arange(plane_count, dtype=jnp.int32)
    scale = 1.0 / jnp.sum(counts).astype(jnp.float32)
    mode_scale = float(MX * MY * MZ) ** (-0.5)
    full_weights = lax.all_gather(spectral_w, "fsdp", axis=0, tiled=True)
    live_count = counts[lane_index]
    coeff_init = jnp.zeros((slot_count, MX * MY * MZ, 2, width), jnp.float32)

    def forward_pass(position, coeff_stack):
        slot_index = slot_order[position]
        grid_field = lax.dynamic_index_in_dim(grid_store, slot_index, 0, keepdims=False)
        grid_coeff = forward_modes(grid_field, x_cells, float(grid_len) ** (-1.5))
        return lax.dynamic_update_index_in_dim(coeff_stack, grid_coeff, position, 0)

    coeff_stack = lax.fori_loop(0, live_count, forward_pass, coeff_init)
    full_coeff = lax.psum(coeff_stack, "fsdp")
    coeff_b = full_coeff.astype(jnp.bfloat16)
    spectrum = mix_modes(coeff_b, full_weights).astype(jnp.bfloat16)

    def backward_pass(position, carry):
        back_stack, local_total = carry
        slot_index = slot_order[position]
        grid_field = lax.dynamic_index_in_dim(grid_store, slot_index, 0, keepdims=False)
        grid_target = lax.dynamic_index_in_dim(target_store, slot_index, 0, keepdims=False)
        grid_spectrum = lax.dynamic_index_in_dim(spectrum, position, 0, keepdims=False)
        branch = inverse_modes(grid_spectrum, x_cells, grid_len)
        d_pre, local_grad = point_part(grid_field, branch, local_w, proj, grid_target, scale)
        grid_back = forward_modes(d_pre, x_cells, mode_scale)
        return (
            lax.dynamic_update_index_in_dim(back_stack, grid_back, position, 0),
            local_total + local_grad,
        )

    back_init = (jnp.zeros_like(coeff_init), jnp.zeros((width, width), jnp.float32))
    back_stack, local_total = lax.fori_loop(0, live_count, backward_pass, back_init)
    grad_part = lax.psum_scatter(
        weight_grad(coeff_b, back_stack), "fsdp", scatter_dimension=0, tiled=True
    )
    grad_spectral = lax.psum(grad_part, "dp")
    grad_local = lax.psum(local_total, ("dp", "fsdp"))
    return (grad_spectral, grad_local)


def solution(mesh):
    return jax.shard_map(
        body,
        mesh=mesh,
        in_specs=(
            P("dp", None, "fsdp", None, None, None),
            P("dp", None, "fsdp", None),
            P("dp", None),
            P(),
            P("fsdp", None, None, None),
            P(),
            P(),
        ),
        out_specs=(P("fsdp", None, None, None), P()),
        check_vma=False,
    )
```

profile of v0, /device:TPU:1, one launch (start us, length us, event | category | flops | bytes accessed | tf_op | source)
XLA Modules:
  0.0 955.1 jit_solution(6195922219674476142)
XLA Ops:
  7.9 1.2 dynamic_slice.42
  9.2 11.0 %while.28 = (s32[]{:T(128)}, f32[6,32,2,128]{3,0,2,1:T(8,128)S(1)}, s32[]{:T(128)}, s32[6]{0:T(128)}, bf16[6,3,48,48,128]{4,3,2,1,0:T(8,128)(2,1)}, /*index=5*/s32[]{:T(128)}, s32[]{:T(128)}, s32[]{:T(128)}, s32[]{:T(128)}) while((s32[]{:T(128)}, f32[6,32,2,128]{3,0,2,1:T(8,128)S(1)}, s32[]{:T(128)}, s32[6]{0:T(128)}, ...), condition=%wide.region_1.2_spmd.clone, body=%wide.region_0.0_spmd.clone.sunk | while | flops 14786103 | bytes 4907401 | solution.py:136
  9.9 1.3 dynamic_slice.73
  13.2 1.9 fusion.419
  15.4 1.9 fusion.421
  21.0 70.6 %all-reduce.11 = bf16[6,32,2,128]{3,0,2,1:T(8,128)(2,1)S(1)} all-reduce(f32[6,32,2,128]{3,0,2,1:T(8,128)S(1)} %get-tuple-element.239), channel_id=1, replica_groups=mesh['dp'=16,'fsdp'=16] {'fsdp'}, use_global_device_ids=true, to_apply=%region_2.3 | all-reduce | flops 49152 | bytes 294912 | tf_op jit(solution)/shard_map/psum | solution.py:137
  92.4 6.0 all-gather.2.cloned.1.call-done
  98.5 2.0 fusion.287
  100.5 2.0 fusion.288
  102.6 34.5 %while.29 = (s32[]{:T(128)}, f32[6,32,2,128]{3,0,2,1:T(8,128)S(1)}, f32[128,128]{1,0:T(8,128)S(1)}, s32[]{:T(128)}, bf16[6,32,2,128]{3,1,2,0:T(8,128)(2,1)S(1)},...) while((s32[]{:T(128)}, f32[6,32,2,128]{3,0,2,1:T(8,128)S(1)}, ...), condition=%wide.region_5.6_spmd.clone, body=%wide.region_4.5_spmd.clone.sunk | while | flops 544574080 | bytes 70409384 | solution.py:156
  105.8 3.1 fusion.474
  109.9 5.0 subtract_multiply_fusion.4
  117.6 1.9 constant_dynamic-slice_fusion.6
  120.8 1.7 copy-done.1
  122.5 3.7 fusion.477
  127.0 5.2 fusion.478
  138.2 3.5 convolution_bitcast_fusion.2
  141.6 2.2 pad_maximum_fusion
  145.8 423.2 %all-reduce.10.cloned.1.call-done = f32[32,2,128,128]{3,2,0,1:T(8,128)} async-done(((f32[32,2,128,128]{3,2,0,1:T(8,128)}), f32[32,2,128,128]{3,2,0,1:T(8,128)}) %all-reduce.10.cloned.1.call-update) | async-done | bytes 4194320
  569.0 1.7 constant_dynamic-slice_fusion.2
  571.3 127.2 %all-reduce.6.cloned.1.call-done = f32[2,2,128,128]{3,2,0,1:T(8,128)} async-done(((f32[2,2,128,128]{3,2,0,1:T(8,128)}), f32[2,2,128,128]{3,2,0,1:T(8,128)}) %all-reduce.6.cloned.1.call-update) | async-done | bytes 262160 | tf_op jit(solution)/shard_map/psum | solution.py:160
  698.5 1.7 copy.102
  700.2 246.9 %all-reduce.8.cloned.1.call-done = f32[128,128]{1,0:T(8,128)} async-done(((f32[128,128]{1,0:T(8,128)}), f32[128,128]{1,0:T(8,128)}) %all-reduce.8.cloned.1.call-update) | async-done | bytes 65552 | tf_op jit(solution)/shard_map/psum | solution.py:161
  947.1 1.5 copy.274
  (85 shorter events, 16.9 us)
Async XLA Ops:
  7.2 91.3 %all-gather.2.cloned.1.call-start = ((), (), s32[]{:S(2)}) async-start(), calls=%async_computation | async-start | bytes 2228224 | tf_op jit(solution)/shard_map/all_gather | solution.py:126
  7.9 561.1 %all-reduce.10.cloned.1.call-start = ((), (), s32[]{:S(2)}) async-start(), calls=%async_computation.3 | async-start | bytes 8388608
  9.2 11.1 %copy-start.5 = (s32[16]{0:T(128)S(1)}, s32[16]{0:T(128)}, u32[]{:S(2)}) copy-start(s32[16]{0:T(128)} %param.15) | copy-start | bytes 196
  20.3 80.2 %copy-start.8 = (bf16[2]{0:T(256)(128)(2,1)S(1)}, bf16[2]{0:T(256)(128)(2,1)}, u32[]{:S(2)}) copy-start(bf16[2]{0:T(256)(128)(2,1)} %constant.200.clone) | copy-start | bytes 16
  91.6 11.0 %copy-start.3 = (bf16[128,128]{1,0:T(8,128)(2,1)S(1)}, bf16[128,128]{1,0:T(8,128)(2,1)}, u32[]{:S(2)}) copy-start(bf16[128,128]{1,0:T(8,128)(2,1)} %param.17) | copy-start | bytes 98308
  91.6 11.0 %copy-start.4 = (f32[128]{0:T(128)S(1)}, f32[128]{0:T(128)}, u32[]{:S(2)}) copy-start(f32[128]{0:T(128)} %param.18) | copy-start | bytes 1540
  91.6 11.0 %copy-start.6 = (s32[6]{0:T(128)S(1)}, s32[6]{0:T(128)}, u32[]{:S(2)}) copy-start(s32[6]{0:T(128)} %get-tuple-element.573) | copy-start | bytes 76
  117.6 2.5 copy-start
  120.8 1.7 copy-start.1
  137.1 6.8 copy-start.2
  143.9 0.7 copy-start.7
  143.9 554.6 %all-reduce.6.cloned.1.call-start = ((), (), s32[]{:S(2)}) async-start(), calls=%async_computation.1 | async-start | bytes 524288 | tf_op jit(solution)/shard_map/psum | solution.py:160
  570.7 376.4 %all-reduce.8.cloned.1.call-start = ((), (), s32[]{:S(2)}) async-start(), calls=%async_computation.2 | async-start | bytes 131072 | tf_op jit(solution)/shard_map/psum | solution.py:161
Sparse Core Ops, SparseCore 0:
  10.6 87.8 all-gather.1
  144.0 424.9 all-reduce.9
  572.2 126.2 all-reduce.5
  704.4 242.6 all-reduce.7
where the time goes:
time: 957 us; the launch traced here: 955 us
  waiting for transfers between devices  805 us (84%)
  blocking collectives  70.6 us (7%)
  matrix products  33.9 us (4%)
  between operations  15.3 us (2%)
  local copies, waits for them, and re-layouts  14 us (1%)
    unnamed x5, waiting for transfers between devices  424 us
    psum x1, waiting for transfers between devices, body(): grad_local = lax.psum(local_total, ('dp', 'fsdp'))  247 us
    psum x1, waiting for transfers between devices, body(): grad_spectral = lax.psum(grad_part, 'dp')  127 us
    psum x1, blocking collectives, body(): full_coeff = lax.psum(coeff_stack, 'fsdp')  70.6 us
  transfers between devices with their start and end apart: 4, of which 4 were waited for; matrix products, arithmetic and copies ran while one was open for 1% of the time, Pallas kernels for 0%

commit v1 on v0

v1 whole, which is shorter than its diff:
```python
import functools
import math

import jax
import jax.numpy as jnp
import numpy as np
from jax import lax
from jax.experimental import pallas as pl
from jax.experimental.pallas import tpu as pltpu
from jax.sharding import PartitionSpec as P

MX, MY, MZ = 4, 4, 2
N_DEV = 16
ROWS = MY * MZ * 2
ROOT_HALF = 0.7071067811865476
INV_ROOT_TWO_PI = 0.3989422804014327
LOG2_E = 1.4426950408889634
MESH = pl.DeviceIdType.MESH
CHUNK = 768


def phases(ids, length):
    product = (ids[:, None] * np.arange(length)[None, :]) % length
    angle = product.astype(np.float32) * np.float32(2.0 * math.pi / length)
    return np.cos(angle).astype(np.float32), np.sin(angle).astype(np.float32)


def split_bf16(values):
    high = values.astype(jnp.bfloat16)
    low = (values - high.astype(np.float32)).astype(jnp.bfloat16)
    return high, low


@functools.lru_cache(maxsize=None)
def tables(length):
    cos_x, sin_x = phases(np.arange(MX) - MX // 2, length)
    cos_y, sin_y = phases(np.arange(MY) - MY // 2, length)
    cos_z, sin_z = phases(np.arange(MZ), length)
    round_z = lambda t: t.astype(jnp.bfloat16).astype(np.float32)

    def product(cz, sz):
        re = cos_y[:, None, :, None] * cz[None, :, None, :] - sin_y[:, None, :, None] * sz[None, :, None, :]
        im = sin_y[:, None, :, None] * cz[None, :, None, :] + cos_y[:, None, :, None] * sz[None, :, None, :]
        shape = (MY, MZ, length * length)
        return re.reshape(shape), -im.reshape(shape)

    re, im = product(round_z(cos_z), round_z(sin_z))
    direct = np.stack([re, im], axis=2).reshape(ROWS, -1)
    turned = np.stack([im, -re], axis=2).reshape(ROWS, -1)
    forward = np.concatenate([*split_bf16(direct), *split_bf16(turned)], axis=0)
    re, im = product(cos_z, sin_z)
    back = np.stack([re, im], axis=2).reshape(ROWS, -1).T * np.float32(float(MX * MY * MZ) ** -0.5)
    high, low = split_bf16(back)
    inverse = np.concatenate([high, low, high], axis=1)
    return np.stack([cos_x, sin_x]).reshape(2, -1), forward, inverse


def times_i(values):
    rows, width = values.shape
    grouped = values.reshape(rows // 8, 8, width)
    even = lax.broadcasted_iota(jnp.int32, grouped.shape, 1) % 2 == 0
    turned = jnp.where(even, -pltpu.roll(grouped, 7, 1), pltpu.roll(grouped, 1, 1))
    return turned.reshape(rows, width)


def dot(a, b):
    return jnp.dot(a, b, preferred_element_type=jnp.float32)


def dot_t(a, b):
    return lax.dot_general(a, b, (((0,), (0,)), ((), ())), preferred_element_type=jnp.float32)


def kernel(
    length, slots, planes,
    fields, cell_table, fwd_table, spec_w, local_w, proj, lists, counts, xphase,
    out_spec, out_local,
    fbuf, rhs, inv_rows, acc, local_acc,
    c_send, c_recv, s_send, s_recv, cg_send, cg_recv, b_send, b_recv, bg_send, bg_recv,
    l_send, l_recv, m_send, m_recv, n_send, n_recv,
    load_sem, send_sem, recv_sem,
):
    cells = length * length
    width = fields.shape[-1]
    rows = slots * 4
    me = {"fsdp": lax.axis_index("fsdp"), "dp": lax.axis_index("dp")}

    def peer_of(axis, t):
        offset = 8 + ((t + 1) // 2) * (1 - 2 * (t % 2))
        return lax.rem(me[axis] + offset, N_DEV)

    def start_exchange(phase, axis, src, dst):
        def one(t, carry):
            peer = peer_of(axis, t)
            pltpu.make_async_remote_copy(
                src_ref=src(peer), dst_ref=dst(me[axis]),
                send_sem=send_sem.at[phase, peer], recv_sem=recv_sem.at[phase, me[axis]],
                device_id={axis: peer}, device_id_type=MESH,
            ).start()
            return carry

        lax.fori_loop(0, N_DEV - 1, one, 0)

    def wait_exchange(phase, axis, src, dst, what):
        def one(t, carry):
            peer = peer_of(axis, t)
            copy = pltpu.make_async_remote_copy(
                src_ref=src(peer), dst_ref=dst(peer),
                send_sem=send_sem.at[phase, peer], recv_sem=recv_sem.at[phase, peer],
                device_id={axis: peer}, device_id_type=MESH,
            )
            (copy.wait_recv if what == "recv" else copy.wait_send)()
            return carry

        lax.fori_loop(0, N_DEV - 1, one, 0)

    part = lambda ref: (lambda peer: ref.at[peer])
    whole = lambda ref: (lambda peer: ref)
    exchanges = {
        0: ("fsdp", part(c_send), part(c_recv)),
        1: ("fsdp", whole(s_send), part(s_recv)),
        2: ("dp", whole(cg_send), part(cg_recv)),
        3: ("fsdp", part(b_send), part(b_recv)),
        4: ("dp", part(l_send), part(l_recv)),
        5: ("dp", whole(bg_send), part(bg_recv)),
        6: ("fsdp", whole(m_send), part(m_recv)),
        7: ("dp", whole(n_send), part(n_recv)),
    }
    start = lambda phase: start_exchange(phase, *exchanges[phase])
    wait_recv = lambda phase: wait_exchange(phase, *exchanges[phase], "recv")
    wait_send = lambda phase: wait_exchange(phase, *exchanges[phase], "send")

    def load(slot):
        return pltpu.make_async_copy(fields.at[slot], fbuf.at[slot], load_sem.at[slot])

    for slot in range(slots):
        load(slot).start()

    barrier = pltpu.get_barrier_semaphore()
    for axis in ("fsdp", "dp"):
        def greet(t, carry, axis=axis):
            pl.semaphore_signal(barrier, inc=1, device_id={axis: peer_of(axis, t)}, device_id_type=MESH)
            return carry

        lax.fori_loop(0, N_DEV - 1, greet, 0)

    def x_phase(part_index, k1, plane):
        return xphase[part_index, k1 * length + me["fsdp"] * planes + plane]

    def fold_modes(slot, plane, product):
        direct = product[0:ROWS] + product[ROWS : 2 * ROWS]
        turned = product[2 * ROWS : 3 * ROWS] + product[3 * ROWS : 4 * ROWS]
        for k1 in range(MX):
            acc[slot, k1] += x_phase(0, k1, plane) * direct + x_phase(1, k1, plane) * turned

    def pack_modes(send):
        for k1 in range(MX):
            for k2 in range(MY):
                pieces = [acc[slot, k1, 4 * k2 : 4 * k2 + 4] for slot in range(slots)]
                send[k1 * MY + k2] = jnp.concatenate(pieces, axis=0)

    acc[...] = jnp.zeros_like(acc)
    for slot in range(slots):
        load(slot).wait()

        def forward_plane(plane, carry, slot=slot):
            fold_modes(slot, plane, dot(fwd_table[...], fbuf[slot, plane]))
            return carry

        lax.fori_loop(0, planes, forward_plane, 0)
    pack_modes(c_send)
    pl.semaphore_wait(barrier, 2 * (N_DEV - 1))
    start(0)
    c_recv[me["fsdp"]] = c_send[me["fsdp"]]

    rhs[...] = jnp.zeros_like(rhs)
    rhs[0:width, 0:width] = local_w[...]
    acc[...] = jnp.zeros_like(acc)
    local_acc[...] = jnp.zeros_like(local_acc)
    s_send[...] = jnp.zeros_like(s_send)
    grid_total = counts[0]
    for lane in range(1, N_DEV):
        grid_total = grid_total + counts[lane]
    scale = 1.0 / (jnp.zeros((1, width), jnp.float32) + grid_total.astype(jnp.float32))
    my_count = counts[me["dp"]]

    wait_recv(0)
    total = c_recv[0]
    for peer in range(1, N_DEV):
        total = total + c_recv[peer]
    coeff = (total * float(length) ** -1.5).astype(jnp.bfloat16)
    coeff_f = coeff.astype(jnp.float32)
    turned = times_i(coeff_f).astype(jnp.bfloat16)
    third = (lax.broadcasted_iota(jnp.int32, (rows, width), 0) // 2) % 2
    mixed = [dot(coeff, spec_w[k3, 0]) + dot(turned, spec_w[k3, 1]) for k3 in range(MZ)]
    s_send[0:rows] = jnp.where(third == 0, mixed[0], mixed[1]).astype(jnp.bfloat16)
    start(1)
    cg_send[...] = coeff_f
    start(2)
    s_recv[me["fsdp"]] = s_send[...]
    cg_recv[me["dp"]] = coeff_f
    wait_recv(1)

    for k1 in range(MX):
        owners = [s_recv[k1 * MY + k2].astype(jnp.float32) for k2 in range(MY)]
        for slot in range(slots):
            piece = jnp.concatenate([o[4 * slot : 4 * slot + 4] for o in owners], axis=0)
            acc_piece = times_i(piece)
            for plane in range(planes):
                term = x_phase(0, k1, plane) * piece + x_phase(1, k1, plane) * acc_piece
                if k1 == 0:
                    inv_rows[slot * planes + plane] = term
                else:
                    inv_rows[slot * planes + plane] += term

    chunks = cells // CHUNK
    picks = lax.broadcasted_iota(jnp.int32, (width, width), 0)

    def point(step, carry):
        unit = step // chunks
        slot, plane, piece = unit // planes, unit % planes, step % chunks
        first = pl.multiple_of(piece * CHUNK, CHUNK)
        live = jnp.int32(0)
        for j in range(slots):
            live = live + jnp.where(jnp.logical_and(lists[0, j] == slot, j < my_count), 1, 0)
        weight = proj[...] * scale * live.astype(jnp.float32)
        values = inv_rows[unit]
        high = values.astype(jnp.bfloat16)
        low = (values - high.astype(jnp.float32)).astype(jnp.bfloat16)
        rhs[width : width + 3 * ROWS, 0:width] = jnp.concatenate([high, high, low], axis=0)
        rhs[width : 2 * width, width : 2 * width] = jnp.where(picks == 3 * ROWS + unit, 1.0, 0.0).astype(jnp.bfloat16)
        field = fbuf[slot, plane, pl.ds(first, CHUNK)]
        left = jnp.concatenate([field, cell_table[pl.ds(first, CHUNK)]], axis=1)
        both = dot(left, rhs[...])
        pre, target = both[:, 0:width], both[:, width : 2 * width]
        gate = 0.5 * lax.erf(pre * ROOT_HALF) + 0.5
        bell = jnp.exp2(pre * pre * (-0.5 * LOG2_E))
        pred = jnp.sum(pre * gate * proj[...], axis=1, keepdims=True)
        slope = gate + pre * (bell * INV_ROOT_TWO_PI)
        d_pre = ((pred - target) * (slope * weight)).astype(jnp.bfloat16)
        local_acc[...] += dot_t(field, d_pre)
        fold_modes(slot, plane, dot(fwd_table[:, pl.ds(first, CHUNK)], d_pre))
        return carry

    lax.fori_loop(0, slots * planes * chunks, point, 0)

    for peer in range(N_DEV):
        l_send[peer] = local_acc[8 * peer : 8 * peer + 8]
    start(4)
    pack_modes(b_send)
    start(3)
    l_recv[me["dp"]] = l_send[me["dp"]]
    b_recv[me["fsdp"]] = b_send[me["fsdp"]]

    def sum_of(ref):
        value = ref[0]
        for peer in range(1, N_DEV):
            value = value + ref[peer]
        return value

    wait_recv(4)
    m_value = sum_of(l_recv)
    m_send[...] = m_value
    start(6)
    m_recv[me["fsdp"]] = m_value
    wait_recv(3)
    b_value = sum_of(b_recv) * float(MX * MY * MZ) ** -0.5
    bg_send[...] = b_value
    start(5)
    bg_recv[me["dp"]] = b_value
    wait_recv(6)
    n_value = sum_of(m_recv)
    n_send[...] = n_value
    start(7)
    n_recv[me["dp"]] = n_value

    wait_recv(2)
    wait_recv(5)
    every = N_DEV * rows
    coeff_all = cg_recv[...].reshape(every, width)
    back_all = bg_recv[...].reshape(every, width)
    third = (lax.broadcasted_iota(jnp.int32, (every, width), 0) // 2) % 2
    left = jnp.concatenate([jnp.where(third == k3, coeff_all, 0.0) for k3 in range(MZ)], axis=1)
    right = jnp.concatenate([back_all, -times_i(back_all)], axis=1)
    right_high = right.astype(jnp.bfloat16)
    right_low = (right - right_high.astype(jnp.float32)).astype(jnp.bfloat16)
    left = left.astype(jnp.bfloat16)
    grad = dot_t(left, right_high) + dot_t(left, right_low)
    for k3 in range(MZ):
        for part_index in range(2):
            out_spec[k3, part_index] = grad[
                k3 * width : (k3 + 1) * width, part_index * width : (part_index + 1) * width
            ]

    wait_recv(7)
    out_local[...] = n_recv[...].reshape(width, width)
    for phase in exchanges:
        wait_send(phase)


def body(fields, targets, lists, counts, spectral_w, local_w, proj):
    _, slots, planes, length, _, width = fields.shape
    cells = length * length
    rows = slots * 4
    xphase, fwd_table, inv_table = tables(length)
    target_rows = targets.reshape(slots * planes, cells).T
    pad = jnp.zeros((cells, width - 3 * ROWS - slots * planes), jnp.bfloat16)
    cell_table = jnp.concatenate([jnp.asarray(inv_table), target_rows, pad], axis=1)
    vmem = pl.BlockSpec(memory_space=pltpu.VMEM)
    smem = pl.BlockSpec(memory_space=pltpu.SMEM)
    f32, bf16 = jnp.float32, jnp.bfloat16
    gathered = pltpu.VMEM((N_DEV, rows, width), f32)
    eighth = pltpu.VMEM((N_DEV, 8, width), f32)
    return pl.pallas_call(
        functools.partial(kernel, length, slots, planes),
        out_shape=(
            jax.ShapeDtypeStruct(spectral_w.shape, f32),
            jax.ShapeDtypeStruct(local_w.shape, f32),
        ),
        in_specs=[pl.BlockSpec(memory_space=pl.ANY)] + [vmem] * 5 + [smem] * 3,
        out_specs=(vmem, vmem),
        scratch_shapes=[
            pltpu.VMEM((slots, planes, cells, width), bf16),
            pltpu.VMEM((2 * width, 2 * width), bf16),
            pltpu.VMEM((slots * planes, ROWS, width), f32),
            pltpu.VMEM((slots, MX, ROWS, width), f32),
            pltpu.VMEM((width, width), f32),
            gathered, gathered,
            pltpu.VMEM((32, width), bf16), pltpu.VMEM((N_DEV, 32, width), bf16),
            pltpu.VMEM((rows, width), f32), gathered,
            gathered, gathered,
            pltpu.VMEM((rows, width), f32), gathered,
            eighth, eighth,
            pltpu.VMEM((8, width), f32), eighth,
            pltpu.VMEM((8, width), f32), eighth,
            pltpu.SemaphoreType.DMA((slots,)),
            pltpu.SemaphoreType.DMA((8, N_DEV)),
            pltpu.SemaphoreType.DMA((8, N_DEV)),
        ],
        compiler_params=pltpu.CompilerParams(
            collective_id=0, has_side_effects=True, vmem_limit_bytes=60 * 1024 * 1024
        ),
        name="fno_step",
    )(
        fields.reshape(slots, planes, cells, width), cell_table, jnp.asarray(fwd_table), spectral_w, local_w,
        proj.reshape(1, width), lists, counts, jnp.asarray(xphase),
    )


def solution(mesh):
    return jax.shard_map(
        body,
        mesh=mesh,
        in_specs=(
            P("dp", None, "fsdp", None, None, None),
            P("dp", None, "fsdp", None),
            P("dp", None),
            P(),
            P("fsdp", None, None, None),
            P(),
            P(),
        ),
        out_specs=(P("fsdp", None, None, None), P()),
        check_vma=False,
    )
```

time: 957 us -> 90.8 us (0.09)
  waiting for transfers between devices: 805 us -> 0 us
  Pallas kernels: 0 us -> 84.2 us
  blocking collectives: 70.6 us -> 0 us
  matrix products: 33.9 us -> 0 us
  between operations: 15.3 us -> 0.66 us
    unnamed x5 -> x0, waiting for transfers between devices: 424 us -> none
    psum x2 -> x0, waiting for transfers between devices: 374 us -> none  [the longest x1 247 us: body(): grad_local = lax.psum(local_total, ('dp', 'fsdp'))]
    pallas_call x0 -> x1, Pallas kernels: none -> 84.2 us  [body(): pl.pallas_call(functools.partial(kernel, length, slots, planes), out_shap...]
    psum x1 -> x0, blocking collectives: 70.6 us -> none  [body(): full_coeff = lax.psum(coeff_stack, 'fsdp')]
    dot_general x37 -> x0, matrix products: 33.9 us -> none  [the longest x24 7.81 us: product(): return jnp.einsum(form, left, right, precision=highest)]
  transfers between devices with their start and end apart: 4 -> 0, of which waited for: 4 -> 0; matrix products, arithmetic and copies ran while one was open for 1% -> 0% of each run, Pallas kernels for 0% -> 0%
where the time goes in v1:
time: 90.8 us; the launch traced here: 90.6 us
  Pallas kernels  84.2 us (93%)
  local copies, waits for them, and re-layouts  4.6 us (5%)
  other arithmetic  1.17 us (1%)
    pallas_call x1, Pallas kernels, body(): pl.pallas_call(functools.partial(kernel, length, slots, planes), out_shap...  84.2 us
    unnamed x4, local copies, waits for them, and re-layouts  3.15 us

profile of v1, /device:TPU:1, one launch (start us, length us, event | category | flops | bytes accessed | tf_op | source)
XLA Modules:
  0.0 90.6 jit_solution(16884479917244252533)
XLA Ops:
  0.6 0.0 copy-start
  0.7 0.1 pad.2.clone
  0.7 1.0 %reshape.14 = bf16[18,2304]{1,0:T(8,128)(2,1)S(1)} reshape(bf16[1,6,3,2304]{3,2,1,0:T(4,128)(2,1)} %param.11) | data formatting | bytes 165888 | tf_op jit(solution)/shard_map/reshape | solution.py:306
  1.8 0.3 copy.13
  2.1 0.0 copy-done
  2.1 1.2 %maximum_maximum_fusion.cell_table = bf16[2304,128]{1,0:T(8,128)(2,1)} fusion(bf16[2304,18]{1,0:T(8,128)(2,1)S(1)} %bitcast.4, bf16[2304,48]{1,0:T(8,128)(2,1)S(1)} %copy-done, bf16[128]{0:T(256)(128)(2,1)S(1)} %pad.2.clone), kind=kLoop, calls=%fused_computation | loop fusion | flops 1769472 | bytes 894208 | tf_op jit(solution)/shard_map/concatenate | solution.py:308
  3.3 84.2 %fno_step.1 = (f32[2,2,128,128]{3,2,1,0:T(8,128)}, f32[128,128]{1,0:T(8,128)}) custom-call(bf16[6,3,2304,128]{3,2,1,0:T(8,128)(2,1)} %bitcast.3, bf16[2304,128]{1,0:T(8,128)(2,1)} %maximum_maximum_fusion.cell_table, bf16[64,2304]{1,0:T(8,128)(2,1)} %constant.9.clone.fwd_table, bf16[2,2,128,128]{3,2,1,0:T(8,128)(2,1)} %spec_w.1, bf16[128,128]{1,0:T(8,128)(2,1)} %local_w.1, ...), custom_call_target="tpu_custom_call" | custom-call | tf_op jit(solution)/shard_map/fno_step/pallas_call | solution.py:314
  87.5 1.7 %copy.16 = f32[2,2,128,128]{3,2,1,0:T(8,128)} copy(f32[2,2,128,128]{3,2,1,0:T(8,128)} %get-tuple-element.4) | data formatting | bytes 524288
  89.2 1.5 %copy.17 = f32[128,128]{1,0:T(8,128)} copy(f32[128,128]{1,0:T(8,128)} %get-tuple-element.5) | data formatting | bytes 131072
  (1 shorter events, 0.0 us)
Async XLA Ops:
  0.6 1.5 %copy-start = (bf16[2304,48]{1,0:T(8,128)(2,1)S(1)}, bf16[2304,48]{1,0:T(8,128)(2,1)}, u32[]{:S(2)}) copy-start(bf16[2304,48]{1,0:T(8,128)(2,1)} %constant.8.clone) | copy-start | bytes 663556

commit v2 on v1

v2 whole, which is shorter than its diff:
```python
import functools
import math

import jax
import jax.numpy as jnp
import numpy as np
from jax import lax
from jax.experimental import pallas as pl
from jax.experimental.pallas import tpu as pltpu
from jax.sharding import PartitionSpec as P

MX, MY, MZ = 4, 4, 2
N_DEV = 16
ROWS = MY * MZ * 2
ROOT_HALF = 0.7071067811865476
INV_ROOT_TWO_PI = 0.3989422804014327
LOG2_E = 1.4426950408889634
MESH = pl.DeviceIdType.MESH
PART = 1152
SHARED = 2


def phases(ids, length):
    product = (ids[:, None] * np.arange(length)[None, :]) % length
    angle = product.astype(np.float32) * np.float32(2.0 * math.pi / length)
    return np.cos(angle).astype(np.float32), np.sin(angle).astype(np.float32)


def split_bf16(values):
    high = values.astype(jnp.bfloat16)
    low = (values - high.astype(np.float32)).astype(jnp.bfloat16)
    return high, low


@functools.lru_cache(maxsize=None)
def tables(length):
    cos_x, sin_x = phases(np.arange(MX) - MX // 2, length)
    cos_y, sin_y = phases(np.arange(MY) - MY // 2, length)
    cos_z, sin_z = phases(np.arange(MZ), length)
    round_z = lambda t: t.astype(jnp.bfloat16).astype(np.float32)

    def product(cz, sz):
        re = cos_y[:, None, :, None] * cz[None, :, None, :] - sin_y[:, None, :, None] * sz[None, :, None, :]
        im = sin_y[:, None, :, None] * cz[None, :, None, :] + cos_y[:, None, :, None] * sz[None, :, None, :]
        shape = (MY, MZ, length * length)
        return re.reshape(shape), -im.reshape(shape)

    re, im = product(round_z(cos_z), round_z(sin_z))
    forward = np.concatenate(split_bf16(np.stack([re, im], axis=2).reshape(ROWS, -1)), axis=0)
    re, im = product(cos_z, sin_z)
    back = np.stack([re, im], axis=2).reshape(ROWS, -1) * np.float32(float(MX * MY * MZ) ** -0.5)
    high, low = split_bf16(back)
    inverse = np.concatenate([high, low, high], axis=0)
    return np.stack([cos_x, sin_x]).reshape(2, -1), forward, inverse


def times_i(values):
    rows, width = values.shape
    grouped = values.reshape(rows // 8, 8, width)
    even = lax.broadcasted_iota(jnp.int32, grouped.shape, 1) % 2 == 0
    turned = jnp.where(even, -pltpu.roll(grouped, 7, 1), pltpu.roll(grouped, 1, 1))
    return turned.reshape(rows, width)


def dot(a, b):
    return jnp.dot(a, b, preferred_element_type=jnp.float32)


def kernel(
    length, slots, planes,
    fields, targets, inv_table, fwd_table, spec_w, local_w, proj, lists, counts, xphase,
    out_spec, out_local,
    fbuf, pbuf, f_share, d_buf, cell_table, rhs, inv_rows, inv_share, tgt, tgt_send, tgt_share, acc, local_acc,
    c_send, c_recv, s_send, s_recv, cg_send, cg_recv, b_send, b_recv, bg_send, bg_recv,
    l_send, l_recv, m_send, m_recv, n_send, n_recv,
    load_sem, send_sem, recv_sem, share_send_sem, share_recv_sem,
):
    cells = length * length
    width = fields.shape[-1]
    rows = slots * 4
    work = slots - SHARED
    units = work * planes
    half = units // 2
    parts = cells // PART
    me = {"fsdp": lax.axis_index("fsdp"), "dp": lax.axis_index("dp")}
    partner = me["dp"] + 1 - 2 * lax.rem(me["dp"], 2)
    order = [lists[0, j] for j in range(slots)]
    my_count, partner_count = counts[me["dp"]], counts[partner]
    mine = my_count > 2
    shared_live = jnp.maximum(my_count, partner_count) > 2

    def peer_of(axis, t):
        offset = 8 + ((t + 1) // 2) * (1 - 2 * (t % 2))
        return lax.rem(me[axis] + offset, N_DEV)

    exchanges = {
        0: ("fsdp", lambda peer: c_send.at[peer], c_recv),
        1: ("fsdp", lambda peer: s_send, s_recv),
        2: ("dp", lambda peer: cg_send, cg_recv),
        3: ("fsdp", lambda peer: b_send.at[peer], b_recv),
        4: ("dp", lambda peer: l_send.at[peer], l_recv),
        5: ("dp", lambda peer: bg_send, bg_recv),
        6: ("fsdp", lambda peer: m_send, m_recv),
        7: ("dp", lambda peer: n_send, n_recv),
    }

    def start(phase):
        axis, src, landing = exchanges[phase]

        def one(t, carry):
            peer = peer_of(axis, t)
            pltpu.make_async_remote_copy(
                src_ref=src(peer), dst_ref=landing.at[me[axis]],
                send_sem=send_sem.at[phase], recv_sem=recv_sem.at[phase],
                device_id={axis: peer}, device_id_type=MESH,
            ).start()
            return carry

        lax.fori_loop(0, N_DEV - 1, one, 0)

    def all_of(phase):
        axis, _, landing = exchanges[phase]
        bytes_of_all = landing.at[pl.ds(0, N_DEV - 1)]
        return pltpu.make_async_remote_copy(
            src_ref=bytes_of_all, dst_ref=bytes_of_all,
            send_sem=send_sem.at[phase], recv_sem=recv_sem.at[phase],
            device_id={axis: peer_of(axis, 0)}, device_id_type=MESH,
        )

    wait_recv = lambda phase: all_of(phase).wait_recv()
    wait_send = lambda phase: all_of(phase).wait_send()

    def share(index, src, dst):
        return pltpu.make_async_remote_copy(
            src_ref=src, dst_ref=dst,
            send_sem=share_send_sem.at[index], recv_sem=share_recv_sem.at[index],
            device_id={"dp": partner}, device_id_type=MESH,
        )

    shares = [
        share(0, tgt_send, tgt_share),
        share(1, pbuf.at[pl.ds(work, SHARED)], f_share),
        share(2, inv_rows.at[pl.ds(units, SHARED * planes)], inv_share),
    ]

    def load(slot):
        return pltpu.make_async_copy(fields.at[slot], fbuf.at[slot], load_sem.at[slot])

    for slot in range(slots):
        load(slot).start()

    barrier = pltpu.get_barrier_semaphore()
    for axis in ("fsdp", "dp"):
        def greet(t, carry, axis=axis):
            pl.semaphore_signal(barrier, inc=1, device_id={axis: peer_of(axis, t)}, device_id_type=MESH)
            return carry

        lax.fori_loop(0, N_DEV - 1, greet, 0)

    def x_phase(part_index, k1, plane):
        return xphase[part_index, k1 * length + me["fsdp"] * planes + plane]

    def fold_modes(slot, plane, product):
        direct = product[0:ROWS] + product[ROWS : 2 * ROWS]
        turned = times_i(direct)
        for k1 in range(MX):
            acc[slot, k1] += x_phase(0, k1, plane) * direct - x_phase(1, k1, plane) * turned

    def pack_modes(send, picks):
        for k1 in range(MX):
            for k2 in range(MY):
                send[k1 * MY + k2] = jnp.concatenate([acc[p, k1, 4 * k2 : 4 * k2 + 4] for p in picks], axis=0)

    acc[...] = jnp.zeros_like(acc)
    for slot in range(slots):
        load(slot).wait()

        def forward_plane(plane, carry, slot=slot):
            fold_modes(slot, plane, dot(fwd_table[...], fbuf[slot, plane]))
            return carry

        lax.fori_loop(0, planes, forward_plane, 0)
    pack_modes(c_send, order)
    pl.semaphore_wait(barrier, 2 * (N_DEV - 1))
    start(0)

    tgt[...] = jnp.zeros_like(tgt)
    tgt_send[...] = jnp.zeros_like(tgt_send)
    for j in range(SHARED):
        tgt_send[planes * j : planes * (j + 1)] = targets[order[work + j]].astype(jnp.float32)
    shares[0].start()

    def by_position(j):
        def one(plane, carry):
            pbuf[j, plane] = fbuf[order[j], plane]
            return carry

        lax.fori_loop(0, planes, one, 0)

    for j in range(work, slots):
        by_position(j)
    shares[1].start()
    c_recv[me["fsdp"]] = c_send[me["fsdp"]]
    for j in range(work):
        tgt[planes * j : planes * (j + 1)] = targets[order[j]].astype(jnp.float32)
        by_position(j)
    rhs[...] = jnp.zeros_like(rhs)
    rhs[0:width, 0:width] = local_w[...]
    acc[...] = jnp.zeros_like(acc)
    local_acc[...] = jnp.zeros_like(local_acc)
    d_buf[...] = jnp.zeros_like(d_buf)
    s_send[...] = jnp.zeros_like(s_send)
    grid_total = counts[0]
    for lane in range(1, N_DEV):
        grid_total = grid_total + counts[lane]
    scale = 1.0 / (jnp.zeros((1, width), jnp.float32) + grid_total.astype(jnp.float32))
    shares[0].wait_recv()
    tgt[half : 2 * half] = jnp.where(mine, tgt[half : 2 * half], tgt_share[0:half])
    cell_rows = jnp.concatenate(
        [inv_table[...], tgt[...].astype(jnp.bfloat16), jnp.zeros((width - 3 * ROWS - 16, cells), jnp.bfloat16)], axis=0
    )
    cell_table[...] = cell_rows.T

    wait_recv(0)
    total = c_recv[0]
    for peer in range(1, N_DEV):
        total = total + c_recv[peer]
    coeff = (total * float(length) ** -1.5).astype(jnp.bfloat16)
    coeff_f = coeff.astype(jnp.float32)
    turned = times_i(coeff_f).astype(jnp.bfloat16)
    third = (lax.broadcasted_iota(jnp.int32, (rows, width), 0) // 2) % 2
    mixed = [dot(coeff, spec_w[k3, 0]) + dot(turned, spec_w[k3, 1]) for k3 in range(MZ)]
    s_send[0:rows] = jnp.where(third == 0, mixed[0], mixed[1]).astype(jnp.bfloat16)
    start(1)
    cg_send[...] = coeff_f
    start(2)
    s_recv[me["fsdp"]] = s_send[...]
    cg_recv[me["dp"]] = coeff_f
    wait_recv(1)

    for k1 in range(MX):
        owners = [s_recv[k1 * MY + k2].astype(jnp.float32) for k2 in range(MY)]
        for j in range(slots):
            piece = jnp.concatenate([o[4 * j : 4 * j + 4] for o in owners], axis=0)
            turned_piece = times_i(piece)
            for plane in range(planes):
                term = x_phase(0, k1, plane) * piece + x_phase(1, k1, plane) * turned_piece
                if k1 == 0:
                    inv_rows[j * planes + plane] = term
                else:
                    inv_rows[j * planes + plane] += term
    shares[2].start()

    picks = lax.broadcasted_iota(jnp.int32, (width, width), 0)

    def reduce_part(unit, part_index):
        slot, plane = unit // planes, unit % planes
        rows_here = pl.ds(part_index * PART, PART)
        left = jnp.concatenate([pbuf[slot, plane, rows_here].T, fwd_table[:, rows_here]], axis=0)
        product = dot(left, d_buf[part_index])
        local_acc[...] += product[0:width]
        fold_modes(slot, plane, product[width:])

    def point(unit, carry):
        @pl.when(unit == half)
        def _():
            shares[1].wait_recv()
            shares[2].wait_recv()
            inv_rows[half:units] = jnp.where(mine, inv_rows[half:units], inv_share[0:half])

            def one(k, carry):
                slot, plane = k // planes, k % planes
                own = pbuf[work // 2 + slot, plane]
                pbuf[work // 2 + slot, plane] = jnp.where(mine, own, f_share[slot, plane])
                return carry

            lax.fori_loop(0, half, one, 0)

        slot, plane = unit // planes, unit % planes
        live = jnp.where(slot < work // 2, jnp.where(slot < my_count, 1, 0), jnp.where(shared_live, 1, 0))
        weight = proj[...] * scale * live.astype(jnp.float32)
        half_proj, half_weight, bell_weight = 0.5 * proj[...], 0.5 * weight, INV_ROOT_TWO_PI * weight
        values = inv_rows[unit]
        high = values.astype(jnp.bfloat16)
        low = (values - high.astype(jnp.float32)).astype(jnp.bfloat16)
        rhs[width : width + 3 * ROWS, 0:width] = jnp.concatenate([high, high, low], axis=0)
        rhs[width : 2 * width, width : 2 * width] = jnp.where(picks == 3 * ROWS + unit, 1.0, 0.0).astype(jnp.bfloat16)
        for part_index in range(parts):
            rows_here = pl.ds(part_index * PART, PART)
            left = jnp.concatenate([pbuf[slot, plane, rows_here], cell_table[rows_here]], axis=1)
            both = dot(left, rhs[...])
            pre, target = both[:, 0:width], both[:, width : 2 * width]
            gate = lax.erf(pre * ROOT_HALF) + 1.0
            bell = jnp.exp2(pre * pre * (-0.5 * LOG2_E))
            pred = jnp.sum(pre * gate * half_proj, axis=1, keepdims=True)
            slope = gate * half_weight + pre * bell * bell_weight
            d_buf[part_index] = ((pred - target) * slope).astype(jnp.bfloat16)
            if part_index == 0:
                reduce_part(jnp.maximum(unit - 1, 0), parts - 1)
            else:
                reduce_part(unit, part_index - 1)
        return carry

    lax.fori_loop(0, units, point, 0)
    reduce_part(units - 1, parts - 1)

    for peer in range(N_DEV):
        l_send[peer] = local_acc[8 * peer : 8 * peer + 8]
    start(4)
    pack_modes(b_send, range(work))
    start(3)
    l_recv[me["dp"]] = l_send[me["dp"]]
    b_recv[me["fsdp"]] = b_send[me["fsdp"]]

    def sum_of(ref):
        value = ref[0]
        for peer in range(1, N_DEV):
            value = value + ref[peer]
        return value

    wait_recv(4)
    m_value = sum_of(l_recv)
    m_send[...] = m_value
    start(6)
    m_recv[me["fsdp"]] = m_value
    wait_recv(3)
    b_value = sum_of(b_recv) * float(MX * MY * MZ) ** -0.5
    bg_send[...] = b_value
    start(5)
    bg_recv[me["dp"]] = b_value

    wait_recv(2)
    near, far = 4 * (work // 2), 4 * work
    pieces = []
    for lane in range(N_DEV):
        kept = jnp.where(counts[lane] > 2, cg_recv[lane, near:far], cg_recv[lane ^ 1, far:rows])
        pieces += [cg_recv[lane, 0:near], kept]
    coeff_all = jnp.concatenate(pieces, axis=0)
    every = N_DEV * far
    third = (lax.broadcasted_iota(jnp.int32, (every, width), 0) // 2) % 2
    left = jnp.concatenate([jnp.where(third == k3, coeff_all, 0.0) for k3 in range(MZ)], axis=1)
    left = left.astype(jnp.bfloat16).T

    wait_recv(6)
    n_value = sum_of(m_recv)
    n_send[...] = n_value
    start(7)
    n_recv[me["dp"]] = n_value

    wait_recv(5)
    back_all = bg_recv[...].reshape(every, width)
    right = jnp.concatenate([back_all, -times_i(back_all)], axis=1)
    right_high = right.astype(jnp.bfloat16)
    right_low = (right - right_high.astype(jnp.float32)).astype(jnp.bfloat16)
    grad = dot(left, right_high) + dot(left, right_low)
    for k3 in range(MZ):
        for part_index in range(2):
            out_spec[k3, part_index] = grad[
                k3 * width : (k3 + 1) * width, part_index * width : (part_index + 1) * width
            ]

    wait_recv(7)
    out_local[...] = n_recv[...].reshape(width, width)
    for phase in exchanges:
        wait_send(phase)
    for one in shares:
        one.wait_send()


def copy_out(spec_in, local_in, out_spec, out_local):
    out_spec[...] = spec_in[...]
    out_local[...] = local_in[...]


def body(fields, targets, lists, counts, spectral_w, local_w, proj):
    _, slots, planes, length, _, width = fields.shape
    cells = length * length
    rows = slots * 4
    work = slots - SHARED
    xphase, fwd_table, inv_table = tables(length)
    vmem = pl.BlockSpec(memory_space=pltpu.VMEM)
    smem = pl.BlockSpec(memory_space=pltpu.SMEM)
    f32, bf16 = jnp.float32, jnp.bfloat16
    coeffs = pltpu.VMEM((N_DEV, rows, width), f32)
    backs = pltpu.VMEM((N_DEV, 4 * work, width), f32)
    eighth = pltpu.VMEM((N_DEV, 8, width), f32)
    results = (
        jax.ShapeDtypeStruct(spectral_w.shape, f32),
        jax.ShapeDtypeStruct(local_w.shape, f32),
    )
    grads = pl.pallas_call(
        functools.partial(kernel, length, slots, planes),
        out_shape=results,
        in_specs=[pl.BlockSpec(memory_space=pl.ANY)] + [vmem] * 6 + [smem] * 3,
        out_specs=(vmem, vmem),
        scratch_shapes=[
            pltpu.VMEM((slots, planes, cells, width), bf16),
            pltpu.VMEM((slots, planes, cells, width), bf16),
            pltpu.VMEM((SHARED, planes, cells, width), bf16),
            pltpu.VMEM((cells // PART, PART, width), bf16),
            pltpu.VMEM((cells, width), bf16),
            pltpu.VMEM((2 * width, 2 * width), bf16),
            pltpu.VMEM((slots * planes, ROWS, width), f32),
            pltpu.VMEM((SHARED * planes, ROWS, width), f32),
            pltpu.VMEM((16, cells), f32), pltpu.VMEM((8, cells), f32), pltpu.VMEM((8, cells), f32),
            pltpu.VMEM((slots, MX, ROWS, width), f32),
            pltpu.VMEM((width, width), f32),
            coeffs, coeffs,
            pltpu.VMEM((32, width), bf16), pltpu.VMEM((N_DEV, 32, width), bf16),
            pltpu.VMEM((rows, width), f32), coeffs,
            backs, backs,
            pltpu.VMEM((4 * work, width), f32), backs,
            eighth, eighth,
            pltpu.VMEM((8, width), f32), eighth,
            pltpu.VMEM((8, width), f32), eighth,
            pltpu.SemaphoreType.DMA((slots,)),
            pltpu.SemaphoreType.DMA((8,)),
            pltpu.SemaphoreType.DMA((8,)),
            pltpu.SemaphoreType.DMA((3,)),
            pltpu.SemaphoreType.DMA((3,)),
        ],
        compiler_params=pltpu.CompilerParams(
            collective_id=0, has_side_effects=True, vmem_limit_bytes=48 * 1024 * 1024
        ),
        name="fno_step",
    )(
        fields.reshape(slots, planes, cells, width), targets.reshape(slots, planes, cells),
        jnp.asarray(inv_table), jnp.asarray(fwd_table), spectral_w, local_w,
        proj.reshape(1, width), lists, counts, jnp.asarray(xphase),
    )
    return pl.pallas_call(
        copy_out, out_shape=results, in_specs=[vmem, vmem], out_specs=(vmem, vmem), name="copy_out",
        compiler_params=pltpu.CompilerParams(vmem_limit_bytes=2 * 1024 * 1024),
    )(*grads)


def solution(mesh):
    return jax.shard_map(
        body,
        mesh=mesh,
        in_specs=(
            P("dp", None, "fsdp", None, None, None),
            P("dp", None, "fsdp", None),
            P("dp", None),
            P(),
            P("fsdp", None, None, None),
            P(),
            P(),
        ),
        out_specs=(P("fsdp", None, None, None), P()),
        check_vma=False,
    )
```

time: 90.8 us -> 62.9 us (0.69)
  Pallas kernels: 84.2 us -> 55 us
  local copies, waits for them, and re-layouts: 4.6 us -> 7.04 us
  other arithmetic: 1.17 us -> 0 us
    pallas_call x1, Pallas kernels: 84.2 us -> 54.2 us  [body(): pl.pallas_call(functools.partial(kernel, length, slots, planes), out_shap...]
    unnamed x4 -> x18, local copies, waits for them, and re-layouts: 3.15 us -> 7.04 us
    reshape x2 -> x0, local copies, waits for them, and re-layouts: 1.37 us -> none  [body(): target_rows = targets.reshape(slots * planes, cells).T]
    concatenate x1 -> x0, other arithmetic: 1.17 us -> none  [body(): jnp.concatenate([jnp.asarray(inv_table), target_rows, pad], axis=1)]
where the time goes in v2:
time: 62.9 us; the launch traced here: 62.7 us
  Pallas kernels  55 us (87%)
  local copies, waits for them, and re-layouts  7.04 us (11%)
  between operations  0.66 us (1%)
    pallas_call x1, Pallas kernels, body(): pl.pallas_call(functools.partial(kernel, length, slots, planes), out_shap...  54.2 us
    unnamed x18, local copies, waits for them, and re-layouts  7.04 us

profile of v2, /device:TPU:1, one launch (start us, length us, event | category | flops | bytes accessed | tf_op | source)
XLA Modules:
  0.0 62.7 jit_solution(17221476797666624034)
XLA Ops:
  0.6 0.0 copy-start
  0.6 0.9 %copy-done = bf16[48,2304]{1,0:T(8,128)(2,1)S(1)} copy-done((bf16[48,2304]{1,0:T(8,128)(2,1)S(1)}, bf16[48,2304]{1,0:T(8,128)(2,1)}, u32[]{:S(2)}) %copy-start) | copy-done | bytes 221208
  1.6 0.0 copy-start.1
  1.6 0.9 %copy-done.1 = bf16[32,2304]{1,0:T(8,128)(2,1)S(1)} copy-done((bf16[32,2304]{1,0:T(8,128)(2,1)S(1)}, bf16[32,2304]{1,0:T(8,128)(2,1)}, u32[]{:S(2)}) %copy-start.1) | copy-done | bytes 147480
  2.5 0.0 copy-start.2
  2.5 0.9 %copy-done.2 = bf16[2,2,128,128]{3,2,1,0:T(8,128)(2,1)S(1)} copy-done((bf16[2,2,128,128]{3,2,1,0:T(8,128)(2,1)S(1)}, bf16[2,2,128,128]{3,2,1,0:T(8,128)(2,1)}, u32[]{:S(2)}) %copy-start.2) | copy-done | bytes 131096
  3.4 0.0 copy-start.3
  3.4 0.9 %copy-done.3 = bf16[1,6,3,2304]{3,2,1,0:T(4,128)(2,1)S(1)} copy-done((bf16[1,6,3,2304]{3,2,1,0:T(4,128)(2,1)S(1)}, bf16[1,6,3,2304]{3,2,1,0:T(4,128)(2,1)}, u32[]{:S(2)}) %copy-start.3) | copy-done | bytes 82968
  4.3 0.0 copy-start.4
  4.3 0.8 %copy-done.4 = bf16[128,128]{1,0:T(8,128)(2,1)S(1)} copy-done((bf16[128,128]{1,0:T(8,128)(2,1)S(1)}, bf16[128,128]{1,0:T(8,128)(2,1)}, u32[]{:S(2)}) %copy-start.4) | copy-done | bytes 32792
  5.0 0.0 copy-start.5
  5.0 0.7 %copy-done.5 = f32[2,192]{1,0:T(2,128)S(1)} copy-done((f32[2,192]{1,0:T(2,128)S(1)}, f32[2,192]{1,0:T(2,128)}, u32[]{:S(2)}) %copy-start.5) | copy-done | bytes 1560
  5.7 0.0 copy-start.6
  5.7 0.7 %copy-done.6 = f32[128]{0:T(128)S(1)} copy-done((f32[128]{0:T(128)S(1)}, f32[128]{0:T(128)}, u32[]{:S(2)}) %copy-start.6) | copy-done | bytes 536
  6.4 0.0 copy-start.7
  6.4 0.7 %copy-done.7 = s32[1,6]{1,0:T(1,128)S(1)} copy-done((s32[1,6]{1,0:T(1,128)S(1)}, s32[1,6]{1,0:T(1,128)}, u32[]{:S(2)}) %copy-start.7) | copy-done | bytes 48
  7.0 0.0 copy-start.8
  7.0 0.7 %copy-done.8 = s32[16]{0:T(128)S(1)} copy-done((s32[16]{0:T(128)S(1)}, s32[16]{0:T(128)}, u32[]{:S(2)}) %copy-start.8) | copy-done | bytes 88
  7.7 54.2 %fno_step.1 = (f32[2,2,128,128]{3,2,1,0:T(8,128)S(1)}, f32[128,128]{1,0:T(8,128)S(1)}) custom-call(bf16[6,3,2304,128]{3,2,1,0:T(8,128)(2,1)} %bitcast.5, bf16[6,3,2304]{2,1,0:T(4,128)(2,1)S(1)} %bitcast.3, bf16[48,2304]{1,0:T(8,128)(2,1)S(1)} %copy-done, bf16[32,2304]{1,0:T(8,128)(2,1)S(1)} %copy-done.1, bf16[2,2,128,128]{3,2,1,0:T(8,128)(2,1)S(1)} %copy-done.2, ...), custom_call_target="tpu_custom_call" | custom-call | tf_op jit(solution)/shard_map/fno_step/pallas_call | solution.py:391
  61.9 0.7 %copy_out.1 = (f32[2,2,128,128]{3,2,1,0:T(8,128)}, f32[128,128]{1,0:T(8,128)}) custom-call(f32[2,2,128,128]{3,2,1,0:T(8,128)S(1)} %get-tuple-element.4.spec_in, f32[128,128]{1,0:T(8,128)S(1)} %get-tuple-element.5.local_in), custom_call_target="tpu_custom_call" | custom-call | tf_op jit(solution)/shard_map/copy_out/pallas_call | solution.py:431
Async XLA Ops:
  0.6 0.9 %copy-start = (bf16[48,2304]{1,0:T(8,128)(2,1)S(1)}, bf16[48,2304]{1,0:T(8,128)(2,1)}, u32[]{:S(2)}) copy-start(bf16[48,2304]{1,0:T(8,128)(2,1)} %constant.6.clone.inv_table) | copy-start | bytes 663556
  1.6 0.9 %copy-start.1 = (bf16[32,2304]{1,0:T(8,128)(2,1)S(1)}, bf16[32,2304]{1,0:T(8,128)(2,1)}, u32[]{:S(2)}) copy-start(bf16[32,2304]{1,0:T(8,128)(2,1)} %constant.7.clone.fwd_table) | copy-start | bytes 442372
  2.5 0.9 %copy-start.2 = (bf16[2,2,128,128]{3,2,1,0:T(8,128)(2,1)S(1)}, bf16[2,2,128,128]{3,2,1,0:T(8,128)(2,1)}, u32[]{:S(2)}) copy-start(bf16[2,2,128,128]{3,2,1,0:T(8,128)(2,1)} %spec_w.1) | copy-start | bytes 393220
  3.4 0.9 %copy-start.3 = (bf16[1,6,3,2304]{3,2,1,0:T(4,128)(2,1)S(1)}, bf16[1,6,3,2304]{3,2,1,0:T(4,128)(2,1)}, u32[]{:S(2)}) copy-start(bf16[1,6,3,2304]{3,2,1,0:T(4,128)(2,1)} %param.11) | copy-start | bytes 248836
  4.3 0.8 %copy-start.4 = (bf16[128,128]{1,0:T(8,128)(2,1)S(1)}, bf16[128,128]{1,0:T(8,128)(2,1)}, u32[]{:S(2)}) copy-start(bf16[128,128]{1,0:T(8,128)(2,1)} %local_w.1) | copy-start | bytes 98308
  5.0 0.7 %copy-start.5 = (f32[2,192]{1,0:T(2,128)S(1)}, f32[2,192]{1,0:T(2,128)}, u32[]{:S(2)}) copy-start(f32[2,192]{1,0:T(2,128)} %constant.8.clone.xphase) | copy-start | bytes 4612
  5.7 0.7 %copy-start.6 = (f32[128]{0:T(128)S(1)}, f32[128]{0:T(128)}, u32[]{:S(2)}) copy-start(f32[128]{0:T(128)} %param.16) | copy-start | bytes 1540
  6.4 0.7 %copy-start.7 = (s32[1,6]{1,0:T(1,128)S(1)}, s32[1,6]{1,0:T(1,128)}, u32[]{:S(2)}) copy-start(s32[1,6]{1,0:T(1,128)} %lists.1) | copy-start | bytes 76
  7.0 0.7 %copy-start.8 = (s32[16]{0:T(128)S(1)}, s32[16]{0:T(128)}, u32[]{:S(2)}) copy-start(s32[16]{0:T(128)} %counts.1) | copy-start | bytes 196

commit v3 on v2

--- a/solution.py
+++ b/solution.py
@@ -17,6 +17,8 @@
 LOG2_E = 1.4426950408889634
 MESH = pl.DeviceIdType.MESH
 PART = 1152
+UNROLL = 2
+INPUTS = 9
 SHARED = 2
 
 
@@ -68,55 +70,55 @@
 
 def kernel(
     length, slots, planes,
-    fields, targets, inv_table, fwd_table, spec_w, local_w, proj, lists, counts, xphase,
-    out_spec, out_local,
+    fields, *rest,
+):
+    inputs, (out_spec, out_local), rest = rest[:INPUTS], rest[INPUTS : INPUTS + 2], rest[INPUTS + 2 :]
+    kept, rest = rest[:INPUTS], rest[INPUTS:]
+    fwd_table, xphase, lists, counts, targets, inv_table, local_w, proj, spec_w = kept
+    (
     fbuf, pbuf, f_share, d_buf, cell_table, rhs, inv_rows, inv_share, tgt, tgt_send, tgt_share, acc, local_acc,
-    c_send, c_recv, s_send, s_recv, cg_send, cg_recv, b_send, b_recv, bg_send, bg_recv,
-    l_send, l_recv, m_send, m_recv, n_send, n_recv,
+    ca_send, ca_recv, cb_send, cb_recv, sa_send, sa_recv, sb_send, sb_recv, cg_send, cg_recv,
+    ba_send, ba_recv, bb_send, bb_recv, bg_send, bg_recv,
+    l_recv, m_send, m_recv, n_send, n_recv,
     load_sem, send_sem, recv_sem, share_send_sem, share_recv_sem,
-):
+    ) = rest
     cells = length * length
     width = fields.shape[-1]
-    rows = slots * 4
+    near = slots - 2 * SHARED
     work = slots - SHARED
     units = work * planes
     half = units // 2
     parts = cells // PART
     me = {"fsdp": lax.axis_index("fsdp"), "dp": lax.axis_index("dp")}
     partner = me["dp"] + 1 - 2 * lax.rem(me["dp"], 2)
-    order = [lists[0, j] for j in range(slots)]
-    my_count, partner_count = counts[me["dp"]], counts[partner]
-    mine = my_count > 2
-    shared_live = jnp.maximum(my_count, partner_count) > 2
+    offsets = [8 + ((t + 1) // 2) * (1 - 2 * (t % 2)) for t in range(N_DEV - 1)]
 
     def peer_of(axis, t):
-        offset = 8 + ((t + 1) // 2) * (1 - 2 * (t % 2))
-        return lax.rem(me[axis] + offset, N_DEV)
+        return lax.rem(me[axis] + offsets[t], N_DEV)
 
     exchanges = {
-        0: ("fsdp", lambda peer: c_send.at[peer], c_recv),
-        1: ("fsdp", lambda peer: s_send, s_recv),
+        0: ("fsdp", lambda peer: ca_send.at[peer], ca_recv),
+        1: ("fsdp", lambda peer: sa_send, sa_recv),
         2: ("dp", lambda peer: cg_send, cg_recv),
-        3: ("fsdp", lambda peer: b_send.at[peer], b_recv),
-        4: ("dp", lambda peer: l_send.at[peer], l_recv),
+        3: ("fsdp", lambda peer: ba_send.at[peer], ba_recv),
+        4: ("dp", lambda peer: local_acc.at[peer], l_recv),
         5: ("dp", lambda peer: bg_send, bg_recv),
         6: ("fsdp", lambda peer: m_send, m_recv),
         7: ("dp", lambda peer: n_send, n_recv),
+        8: ("fsdp", lambda peer: cb_send.at[peer], cb_recv),
+        9: ("fsdp", lambda peer: sb_send, sb_recv),
+        10: ("fsdp", lambda peer: bb_send.at[peer], bb_recv),
     }
 
     def start(phase):
         axis, src, landing = exchanges[phase]
-
-        def one(t, carry):
+        for t in range(N_DEV - 1):
             peer = peer_of(axis, t)
             pltpu.make_async_remote_copy(
                 src_ref=src(peer), dst_ref=landing.at[me[axis]],
                 send_sem=send_sem.at[phase], recv_sem=recv_sem.at[phase],
                 device_id={axis: peer}, device_id_type=MESH,
             ).start()
-            return carry
-
-        lax.fori_loop(0, N_DEV - 1, one, 0)
 
     def all_of(phase):
         axis, _, landing = exchanges[phase]
@@ -146,16 +148,20 @@
     def load(slot):
         return pltpu.make_async_copy(fields.at[slot], fbuf.at[slot], load_sem.at[slot])
 
+    fetches = [
+        pltpu.make_async_copy(src, dst, load_sem.at[slots + index]) for index, (src, dst) in enumerate(zip(inputs, kept))
+    ]
+    for fetch in fetches[:4]:
+        fetch.start()
     for slot in range(slots):
         load(slot).start()
+    for fetch in fetches[4:]:
+        fetch.start()
 
     barrier = pltpu.get_barrier_semaphore()
-    for axis in ("fsdp", "dp"):
-        def greet(t, carry, axis=axis):
+    for t in range(N_DEV - 1):
+        for axis in ("fsdp", "dp"):
             pl.semaphore_signal(barrier, inc=1, device_id={axis: peer_of(axis, t)}, device_id_type=MESH)
-            return carry
-
-        lax.fori_loop(0, N_DEV - 1, greet, 0)
 
     def x_phase(part_index, k1, plane):
         return xphase[part_index, k1 * length + me["fsdp"] * planes + plane]
@@ -172,6 +178,13 @@
                 send[k1 * MY + k2] = jnp.concatenate([acc[p, k1, 4 * k2 : 4 * k2 + 4] for p in picks], axis=0)
 
     acc[...] = jnp.zeros_like(acc)
+    for fetch in fetches[:4]:
+        fetch.wait()
+    order = [lists[0, j] for j in range(slots)]
+    my_count, partner_count = counts[me["dp"]], counts[partner]
+    mine = my_count > 2
+    shared_live = jnp.maximum(my_count, partner_count) > 2
+
     for slot in range(slots):
         load(slot).wait()
 
@@ -180,10 +193,14 @@
             return carry
 
         lax.fori_loop(0, planes, forward_plane, 0)
-    pack_modes(c_send, order)
+    pack_modes(ca_send, order[:near])
     pl.semaphore_wait(barrier, 2 * (N_DEV - 1))
     start(0)
-
+    pack_modes(cb_send, order[near:])
+    start(8)
+
+    for fetch in fetches[4:]:
+        fetch.wait()
     tgt[...] = jnp.zeros_like(tgt)
     tgt_send[...] = jnp.zeros_like(tgt_send)
     for j in range(SHARED):
@@ -200,7 +217,8 @@
     for j in range(work, slots):
         by_position(j)
     shares[1].start()
-    c_recv[me["fsdp"]] = c_send[me["fsdp"]]
+    ca_recv[me["fsdp"]] = ca_send[me["fsdp"]]
+    cb_recv[me["fsdp"]] = cb_send[me["fsdp"]]
     for j in range(work):
         tgt[planes * j : planes * (j + 1)] = targets[order[j]].astype(jnp.float32)
         by_position(j)
@@ -209,7 +227,6 @@
     acc[...] = jnp.zeros_like(acc)
     local_acc[...] = jnp.zeros_like(local_acc)
     d_buf[...] = jnp.zeros_like(d_buf)
-    s_send[...] = jnp.zeros_like(s_send)
     grid_total = counts[0]
     for lane in range(1, N_DEV):
         grid_total = grid_total + counts[lane]
@@ -221,35 +238,49 @@
     )
     cell_table[...] = cell_rows.T
 
+    def sum_of(ref):
+        value = ref[0]
+        for peer in range(1, N_DEV):
+            value = value + ref[peer]
+        return value
+
+    def mix(landing, send):
+        coeff = (sum_of(landing) * float(length) ** -1.5).astype(jnp.bfloat16)
+        coeff_f = coeff.astype(jnp.float32)
+        turned = times_i(coeff_f).astype(jnp.bfloat16)
+        third = (lax.broadcasted_iota(jnp.int32, coeff.shape, 0) // 2) % 2
+        mixed = [dot(coeff, spec_w[k3, 0]) + dot(turned, spec_w[k3, 1]) for k3 in range(MZ)]
+        send[...] = jnp.where(third == 0, mixed[0], mixed[1]).astype(jnp.bfloat16)
+        return coeff_f
+
     wait_recv(0)
-    total = c_recv[0]
-    for peer in range(1, N_DEV):
-        total = total + c_recv[peer]
-    coeff = (total * float(length) ** -1.5).astype(jnp.bfloat16)
-    coeff_f = coeff.astype(jnp.float32)
-    turned = times_i(coeff_f).astype(jnp.bfloat16)
-    third = (lax.broadcasted_iota(jnp.int32, (rows, width), 0) // 2) % 2
-    mixed = [dot(coeff, spec_w[k3, 0]) + dot(turned, spec_w[k3, 1]) for k3 in range(MZ)]
-    s_send[0:rows] = jnp.where(third == 0, mixed[0], mixed[1]).astype(jnp.bfloat16)
+    coeff_near = mix(ca_recv, sa_send)
     start(1)
-    cg_send[...] = coeff_f
+    wait_recv(8)
+    coeff_far = mix(cb_recv, sb_send)
+    start(9)
+    cg_send[...] = jnp.concatenate([coeff_near, coeff_far], axis=0)
     start(2)
-    s_recv[me["fsdp"]] = s_send[...]
-    cg_recv[me["dp"]] = coeff_f
+    sa_recv[me["fsdp"]] = sa_send[...]
+    sb_recv[me["fsdp"]] = sb_send[...]
+    cg_recv[me["dp"]] = cg_send[...]
+
+    def inverse_rows(landing, first, last):
+        for k1 in range(MX):
+            owners = [landing[k1 * MY + k2].astype(jnp.float32) for k2 in range(MY)]
+            for j in range(last - first):
+                piece = jnp.concatenate([o[4 * j : 4 * j + 4] for o in owners], axis=0)
+                turned_piece = times_i(piece)
+                for plane in range(planes):
+                    term = x_phase(0, k1, plane) * piece + x_phase(1, k1, plane) * turned_piece
+                    unit = (first + j) * planes + plane
+                    if k1 == 0:
+                        inv_rows[unit] = term
+                    else:
+                        inv_rows[unit] += term
+
     wait_recv(1)
-
-    for k1 in range(MX):
-        owners = [s_recv[k1 * MY + k2].astype(jnp.float32) for k2 in range(MY)]
-        for j in range(slots):
-            piece = jnp.concatenate([o[4 * j : 4 * j + 4] for o in owners], axis=0)
-            turned_piece = times_i(piece)
-            for plane in range(planes):
-                term = x_phase(0, k1, plane) * piece + x_phase(1, k1, plane) * turned_piece
-                if k1 == 0:
-                    inv_rows[j * planes + plane] = term
-                else:
-                    inv_rows[j * planes + plane] += term
-    shares[2].start()
+    inverse_rows(sa_recv, 0, near)
 
     picks = lax.broadcasted_iota(jnp.int32, (width, width), 0)
 
@@ -258,26 +289,12 @@
         rows_here = pl.ds(part_index * PART, PART)
         left = jnp.concatenate([pbuf[slot, plane, rows_here].T, fwd_table[:, rows_here]], axis=0)
         product = dot(left, d_buf[part_index])
-        local_acc[...] += product[0:width]
+        local_acc[...] += product[0:width].reshape(local_acc.shape)
         fold_modes(slot, plane, product[width:])
 
-    def point(unit, carry):
-        @pl.when(unit == half)
-        def _():
-            shares[1].wait_recv()
-            shares[2].wait_recv()
-            inv_rows[half:units] = jnp.where(mine, inv_rows[half:units], inv_share[0:half])
-
-            def one(k, carry):
-                slot, plane = k // planes, k % planes
-                own = pbuf[work // 2 + slot, plane]
-                pbuf[work // 2 + slot, plane] = jnp.where(mine, own, f_share[slot, plane])
-                return carry
-
-            lax.fori_loop(0, half, one, 0)
-
+    def point(unit):
         slot, plane = unit // planes, unit % planes
-        live = jnp.where(slot < work // 2, jnp.where(slot < my_count, 1, 0), jnp.where(shared_live, 1, 0))
+        live = jnp.where(slot < near, jnp.where(slot < my_count, 1, 0), jnp.where(shared_live, 1, 0))
         weight = proj[...] * scale * live.astype(jnp.float32)
         half_proj, half_weight, bell_weight = 0.5 * proj[...], 0.5 * weight, INV_ROOT_TWO_PI * weight
         values = inv_rows[unit]
@@ -299,42 +316,67 @@
                 reduce_part(jnp.maximum(unit - 1, 0), parts - 1)
             else:
                 reduce_part(unit, part_index - 1)
+
+    def step(index, carry):
+        first = index * UNROLL
+
+        @pl.when(first == 4)
+        def _():
+            wait_recv(9)
+            inverse_rows(sb_recv, near, slots)
+            shares[2].start()
+
+        @pl.when(first == half)
+        def _():
+            shares[1].wait_recv()
+            shares[2].wait_recv()
+            inv_rows[half:units] = jnp.where(mine, inv_rows[half:units], inv_share[0:half])
+
+            def one(k, carry):
+                slot, plane = k // planes, k % planes
+                pbuf[near + slot, plane] = jnp.where(mine, pbuf[near + slot, plane], f_share[slot, plane])
+                return carry
+
+            lax.fori_loop(0, half, one, 0)
+
+        @pl.when(first == half + 2)
+        def _():
+            pack_modes(ba_send, range(near))
+            start(3)
+            ba_recv[me["fsdp"]] = ba_send[me["fsdp"]]
+
+        for sub in range(UNROLL):
+            point(first + sub)
         return carry
 
-    lax.fori_loop(0, units, point, 0)
+    lax.fori_loop(0, units // UNROLL, step, 0)
     reduce_part(units - 1, parts - 1)
 
-    for peer in range(N_DEV):
-        l_send[peer] = local_acc[8 * peer : 8 * peer + 8]
     start(4)
-    pack_modes(b_send, range(work))
-    start(3)
-    l_recv[me["dp"]] = l_send[me["dp"]]
-    b_recv[me["fsdp"]] = b_send[me["fsdp"]]
-
-    def sum_of(ref):
-        value = ref[0]
-        for peer in range(1, N_DEV):
-            value = value + ref[peer]
-        return value
+    pack_modes(bb_send, range(near, work))
+    start(10)
+    l_recv[me["dp"]] = local_acc[me["dp"]]
+    bb_recv[me["fsdp"]] = bb_send[me["fsdp"]]
+    back_scale = float(MX * MY * MZ) ** -0.5
+    wait_recv(3)
+    near_value = sum_of(ba_recv) * back_scale
 
     wait_recv(4)
     m_value = sum_of(l_recv)
     m_send[...] = m_value
     start(6)
     m_recv[me["fsdp"]] = m_value
-    wait_recv(3)
-    b_value = sum_of(b_recv) * float(MX * MY * MZ) ** -0.5
-    bg_send[...] = b_value
+    wait_recv(10)
+    bg_send[...] = jnp.concatenate([near_value, sum_of(bb_recv) * back_scale], axis=0)
     start(5)
-    bg_recv[me["dp"]] = b_value
+    bg_recv[me["dp"]] = bg_send[...]
 
     wait_recv(2)
-    near, far = 4 * (work // 2), 4 * work
+    first, far = 4 * near, 4 * work
     pieces = []
     for lane in range(N_DEV):
-        kept = jnp.where(counts[lane] > 2, cg_recv[lane, near:far], cg_recv[lane ^ 1, far:rows])
-        pieces += [cg_recv[lane, 0:near], kept]
+        taken = jnp.where(counts[lane] > 2, cg_recv[lane, first:far], cg_recv[lane ^ 1, far : 4 * slots])
+        pieces += [cg_recv[lane, 0:first], taken]
     coeff_all = jnp.concatenate(pieces, axis=0)
     every = N_DEV * far
     third = (lax.broadcasted_iota(jnp.int32, (every, width), 0) // 2) % 2
@@ -375,25 +417,29 @@
 def body(fields, targets, lists, counts, spectral_w, local_w, proj):
     _, slots, planes, length, _, width = fields.shape
     cells = length * length
-    rows = slots * 4
-    work = slots - SHARED
+    work, near = slots - SHARED, slots - 2 * SHARED
     xphase, fwd_table, inv_table = tables(length)
     vmem = pl.BlockSpec(memory_space=pltpu.VMEM)
-    smem = pl.BlockSpec(memory_space=pltpu.SMEM)
     f32, bf16 = jnp.float32, jnp.bfloat16
-    coeffs = pltpu.VMEM((N_DEV, rows, width), f32)
-    backs = pltpu.VMEM((N_DEV, 4 * work, width), f32)
-    eighth = pltpu.VMEM((N_DEV, 8, width), f32)
     results = (
         jax.ShapeDtypeStruct(spectral_w.shape, f32),
         jax.ShapeDtypeStruct(local_w.shape, f32),
     )
+    fixed = (
+        jnp.asarray(fwd_table), jnp.asarray(xphase), lists, counts, targets.reshape(slots, planes, cells),
+        jnp.asarray(inv_table), local_w, proj.reshape(1, width), spectral_w,
+    )
+    in_smem = (1, 2, 3)
+    eight = pltpu.VMEM((N_DEV, 8, width), f32)
+    sixteen = pltpu.VMEM((N_DEV, 4 * (slots - near), width), f32)
+    hbm = pl.BlockSpec(memory_space=pltpu.HBM)
     grads = pl.pallas_call(
         functools.partial(kernel, length, slots, planes),
-        out_shape=results,
-        in_specs=[pl.BlockSpec(memory_space=pl.ANY)] + [vmem] * 6 + [smem] * 3,
+        out_shape=tuple(pltpu.VMEM(r.shape, r.dtype) for r in results),
+        in_specs=[hbm] * (1 + INPUTS),
         out_specs=(vmem, vmem),
         scratch_shapes=[
+            *((pltpu.SMEM if index in in_smem else pltpu.VMEM)(a.shape, a.dtype) for index, a in enumerate(fixed)),
             pltpu.VMEM((slots, planes, cells, width), bf16),
             pltpu.VMEM((slots, planes, cells, width), bf16),
             pltpu.VMEM((SHARED, planes, cells, width), bf16),
@@ -404,18 +450,19 @@
             pltpu.VMEM((SHARED * planes, ROWS, width), f32),
             pltpu.VMEM((16, cells), f32), pltpu.VMEM((8, cells), f32), pltpu.VMEM((8, cells), f32),
             pltpu.VMEM((slots, MX, ROWS, width), f32),
-            pltpu.VMEM((width, width), f32),
-            coeffs, coeffs,
-            pltpu.VMEM((32, width), bf16), pltpu.VMEM((N_DEV, 32, width), bf16),
-            pltpu.VMEM((rows, width), f32), coeffs,
-            backs, backs,
-            pltpu.VMEM((4 * work, width), f32), backs,
-            eighth, eighth,
-            pltpu.VMEM((8, width), f32), eighth,
-            pltpu.VMEM((8, width), f32), eighth,
-            pltpu.SemaphoreType.DMA((slots,)),
-            pltpu.SemaphoreType.DMA((8,)),
-            pltpu.SemaphoreType.DMA((8,)),
+            pltpu.VMEM((N_DEV, width // N_DEV, width), f32),
+            eight, eight, sixteen, sixteen,
+            pltpu.VMEM((8, width), bf16), pltpu.VMEM((N_DEV, 8, width), bf16),
+            pltpu.VMEM((16, width), bf16), pltpu.VMEM((N_DEV, 16, width), bf16),
+            pltpu.VMEM((4 * slots, width), f32), pltpu.VMEM((N_DEV, 4 * slots, width), f32),
+            eight, eight, eight, eight,
+            pltpu.VMEM((4 * work, width), f32), pltpu.VMEM((N_DEV, 4 * work, width), f32),
+            eight,
+            pltpu.VMEM((8, width), f32), eight,
+            pltpu.VMEM((8, width), f32), eight,
+            pltpu.SemaphoreType.DMA((slots + INPUTS,)),
+            pltpu.SemaphoreType.DMA((11,)),
+            pltpu.SemaphoreType.DMA((11,)),
             pltpu.SemaphoreType.DMA((3,)),
             pltpu.SemaphoreType.DMA((3,)),
         ],
@@ -423,11 +470,7 @@
             collective_id=0, has_side_effects=True, vmem_limit_bytes=48 * 1024 * 1024
         ),
         name="fno_step",
-    )(
-        fields.reshape(slots, planes, cells, width), targets.reshape(slots, planes, cells),
-        jnp.asarray(inv_table), jnp.asarray(fwd_table), spectral_w, local_w,
-        proj.reshape(1, width), lists, counts, jnp.asarray(xphase),
-    )
+    )(*(pltpu.with_memory_space_constraint(a, pltpu.HBM) for a in (fields.reshape(slots, planes, cells, width), *fixed)))
     return pl.pallas_call(
         copy_out, out_shape=results, in_specs=[vmem, vmem], out_specs=(vmem, vmem), name="copy_out",
         compiler_params=pltpu.CompilerParams(vmem_limit_bytes=2 * 1024 * 1024),

time: 62.9 us -> 54.3 us (0.86)
  local copies, waits for them, and re-layouts: 7.04 us -> 0 us
  Pallas kernels: 55 us -> 53.6 us
    unnamed x18 -> x0, local copies, waits for them, and re-layouts: 7.04 us -> none
    pallas_call x1, Pallas kernels: 54.2 us -> 52.8 us  [body(): pl.pallas_call(functools.partial(kernel, length, slots, planes), out_shap...]
where the time goes in v3:
time: 54.3 us; the launch traced here: 54.2 us
  Pallas kernels  53.6 us (99%)
  between operations  0.64 us (1%)
    pallas_call x1, Pallas kernels, body(): pl.pallas_call(functools.partial(kernel, length, slots, planes), out_shap...  52.8 us

profile of v3, /device:TPU:1, one launch (start us, length us, event | category | flops | bytes accessed | tf_op | source)
XLA Modules:
  0.0 54.2 jit_solution(18161792393118521900)
XLA Ops:
  0.6 52.8 %fno_step.1 = (f32[2,2,128,128]{3,2,1,0:T(8,128)S(1)}, f32[128,128]{1,0:T(8,128)S(1)}) custom-call(bf16[6,3,2304,128]{3,2,1,0:T(8,128)(2,1)} %bitcast.3, bf16[32,2304]{1,0:T(8,128)(2,1)} %constant.6.clone.rest_0_, f32[2,192]{1,0:T(2,128)} %constant.7.clone.rest_1_, s32[1,6]{1,0:T(1,128)} %rest_2_.1, s32[16]{0:T(128)} %rest_3_.1, ...), custom_call_target="tpu_custom_call" | custom-call | tf_op jit(solution)/shard_map/fno_step/pallas_call | solution.py:436
  53.5 0.7 %copy_out.1 = (f32[2,2,128,128]{3,2,1,0:T(8,128)}, f32[128,128]{1,0:T(8,128)}) custom-call(f32[2,2,128,128]{3,2,1,0:T(8,128)S(1)} %get-tuple-element.4.spec_in, f32[128,128]{1,0:T(8,128)S(1)} %get-tuple-element.5.local_in), custom_call_target="tpu_custom_call" | custom-call | tf_op jit(solution)/shard_map/copy_out/pallas_call | solution.py:474
